TPU v7x, 32 devices: a whole 2x2x4 slice. The times are simulated.
32 devices in a mesh: dp: 4 (over x, core), ctx: 4 (over z), tensor: 2 (over y).
Axes of the slice: x: 2, y: 2, z: 4, core: 2. Of those that a mesh axis runs over, the one named last changes fastest.
Arguments:
- inputs: bfloat16 [8192, 768], P(('dp', 'ctx')), may hold values from -6 to 6
- segments: int32 [4, 2048], P('dp', 'ctx'), may hold values from 0 to 7, never falling along the last dimension, each value on 1 to 1536 neighbouring positions
- query_proj: bfloat16 [768, 768], P(None, 'tensor'), may hold values from -0.4375 to 0.4375
- key_proj: bfloat16 [768, 768], P(None, 'tensor'), may hold values from -0.21875 to 0.21875
- value_proj: bfloat16 [768, 768], P(None, 'tensor'), may hold values from -0.21875 to 0.21875
- query_bias: bfloat16 [768], P('tensor'), may hold values from -3 to 3
- value_bias: bfloat16 [768], P('tensor'), may hold values from -0.59765625 to 0.59765625
- output_proj: bfloat16 [768, 768], P('tensor'), may hold values from -0.875 to 0.875
- output_bias: bfloat16 [768], replicated, may hold values from -1.1953125 to 1.1953125
- attn_gain: bfloat16 [768], replicated, may hold values from 0.5 to 1.5
- attn_shift: bfloat16 [768], replicated, may hold values from -1.1953125 to 1.1953125
- expand_proj: bfloat16 [768, 3072], P(None, 'tensor'), may hold values from -0.21875 to 0.21875
- expand_bias: bfloat16 [3072], P('tensor'), may hold values from -3 to 3
- shrink_proj: bfloat16 [3072, 768], P('tensor'), may hold values from -0.109375 to 0.109375
- shrink_bias: bfloat16 [768], replicated, may hold values from -1.1953125 to 1.1953125
- final_gain: bfloat16 [768], replicated, may hold values from 0.5 to 1.5
- final_shift: bfloat16 [768], replicated, may hold values from -1.1953125 to 1.1953125
- cotangent: bfloat16 [8192, 768], P(('dp', 'ctx')), may hold values from -6 to 6
Outputs:
- output: bfloat16 [8192, 768], P(('dp', 'ctx'))
- input_grad: float32 [8192, 768], P(('dp', 'ctx'))
- query_grad: float32 [768, 768], P(None, 'tensor')
- key_grad: float32 [768, 768], P(None, 'tensor')
- value_grad: float32 [768, 768], P(None, 'tensor')
- qbias_grad: float32 [768], P('tensor')
- vbias_grad: float32 [768], P('tensor')
- oproj_grad: float32 [768, 768], P('tensor')
- obias_grad: float32 [768], replicated
- again_grad: float32 [768], replicated
- ashift_grad: float32 [768], replicated
- expand_grad: float32 [768, 3072], P(None, 'tensor')
- ebias_grad: float32 [3072], P('tensor')
- shrink_grad: float32 [3072, 768], P('tensor')
- sbias_grad: float32 [768], replicated
- fgain_grad: float32 [768], replicated
- fshift_grad: float32 [768], replicated
Inputs may be any that keep to these rules, and one draw needn't show every extreme that they name: `segments`: along each sequence the ids never fall; every id from 0 to 7 names one document of the sequence, and one document has 1536 tokens.
All inputs are finite; a program needn't handle non-finite values.
Results may differ from a plain program's by a relative error of at most 0.019.
Values may be sent and summed in bfloat16 or wider, within the bound.
A program may use at most 256 MiB of HBM per device.

v0:
```python
import jax
import jax.numpy as jnp
from jax import lax
from jax.sharding import PartitionSpec as P

HEAD_DIM = 64
norm_eps = 1e-12
masked = -1e30
contract_rows = (((0,), (0,)), ((), ()))
contract_cols = (((1,), (1,)), ((), ()))


def matmul(left, right):
    return jnp.dot(left, right, preferred_element_type=jnp.float32)


def inner_rows(left, right):
    return lax.dot_general(left, right, contract_rows, preferred_element_type=jnp.float32)


def inner_cols(left, right):
    return lax.dot_general(left, right, contract_cols, preferred_element_type=jnp.float32)


def norm_forward(values, gain, shift):
    centred = values - jnp.mean(values, axis=-1, keepdims=True)
    spread = jnp.mean(centred * centred, axis=-1, keepdims=True)
    recip = lax.rsqrt(spread + norm_eps)
    normed = centred * recip
    return (normed * gain + shift, normed, recip)


def norm_backward(upstream, normed, recip, gain):
    scaled = upstream * gain
    centred = (
        scaled
        - jnp.mean(scaled, axis=-1, keepdims=True)
        - normed * jnp.mean(scaled * normed, axis=-1, keepdims=True)
    )
    return (centred * recip, jnp.sum(upstream * normed, axis=0), jnp.sum(upstream, axis=0))


def cross_scores(left, right):
    return inner_cols(left, right)


def spread_apply(weights_in, right):
    return matmul(weights_in, right)


def spread_transpose(weights_in, left):
    return inner_rows(weights_in, left)


def body(
    inputs,
    segments,
    query_proj,
    key_proj,
    value_proj,
    query_bias,
    value_bias,
    output_proj,
    output_bias,
    attn_gain,
    attn_shift,
    expand_proj,
    expand_bias,
    shrink_proj,
    shrink_bias,
    final_gain,
    final_shift,
    cotangent,
):
    head_count = query_proj.shape[1] // HEAD_DIM
    scale = HEAD_DIM ** (-0.5)
    seg_local = segments[0]
    queries = (matmul(inputs, query_proj) + query_bias.astype(jnp.float32)).astype(jnp.bfloat16)
    keys = matmul(inputs, key_proj).astype(jnp.bfloat16)
    values = (matmul(inputs, value_proj) + value_bias.astype(jnp.float32)).astype(jnp.bfloat16)
    all_keys, all_values, key_ids = (
        lax.all_gather(keys, "ctx", axis=0, tiled=True),
        lax.all_gather(values, "ctx", axis=0, tiled=True),
        lax.all_gather(seg_local.astype(jnp.bfloat16), "ctx", axis=0, tiled=True),
    )
    query_segs = seg_local.astype(jnp.float32)
    key_segs = key_ids.astype(jnp.float32)
    same_seg = query_segs[:, None] == key_segs[None, :]

    def split_heads(matrix):
        return jnp.swapaxes(matrix.reshape(matrix.shape[0], head_count, HEAD_DIM), 0, 1)

    def join_heads(stack):
        return jnp.swapaxes(stack, 0, 1).reshape(stack.shape[1], head_count * HEAD_DIM)

    query_heads = split_heads(queries)
    key_heads = split_heads(all_keys)
    value_heads = split_heads(all_values)

    def head_forward(state, triple):
        query_head, key_head, value_head = triple
        scores = cross_scores(query_head, key_head) * scale
        scores = jnp.where(same_seg, scores, masked)
        row_max = jnp.max(scores, axis=1, keepdims=True)
        exp_scores = jnp.where(same_seg, jnp.exp(scores - row_max), 0.0)
        row_sum = jnp.sum(exp_scores, axis=1, keepdims=True)
        attn_probs = (exp_scores / row_sum).astype(jnp.bfloat16)
        mixed = spread_apply(attn_probs, value_head)
        return (state, (mixed, row_max + jnp.log(row_sum)))

    mixed_heads, log_sums = lax.scan(head_forward, None, (query_heads, key_heads, value_heads))[1]
    attended = join_heads(mixed_heads).astype(jnp.bfloat16)
    attn_total = lax.psum(matmul(attended, output_proj).astype(jnp.bfloat16), "tensor").astype(
        jnp.float32
    )
    attn_gain_f = attn_gain.astype(jnp.float32)
    first, first_normed, first_recip = norm_forward(
        inputs.astype(jnp.float32) + attn_total + output_bias.astype(jnp.float32),
        attn_gain_f,
        attn_shift.astype(jnp.float32),
    )
    first_low = first.astype(jnp.bfloat16)
    pre_act = matmul(first_low, expand_proj) + expand_bias.astype(jnp.float32)
    activated, gelu_back = jax.vjp(lambda pre_in: jax.nn.gelu(pre_in, approximate=False), pre_act)
    hidden = activated.astype(jnp.bfloat16)
    feed_total = lax.psum(matmul(hidden, shrink_proj).astype(jnp.bfloat16), "tensor").astype(
        jnp.float32
    )
    second = first + feed_total + shrink_bias.astype(jnp.float32)
    final_gain_f = final_gain.astype(jnp.float32)
    output, second_normed, second_recip = norm_forward(
        second, final_gain_f, final_shift.astype(jnp.float32)
    )
    upstream = cotangent.astype(jnp.float32)
    grad_second, fgain_grad, fshift_grad = norm_backward(
        upstream, second_normed, second_recip, final_gain_f
    )
    sbias_grad = jnp.sum(grad_second, axis=0)
    grad_second_low = grad_second.astype(jnp.bfloat16)
    shrink_grad = inner_rows(hidden, grad_second_low)
    grad_act = inner_cols(grad_second_low, shrink_proj)
    grad_pre = gelu_back(grad_act)[0].astype(jnp.bfloat16)
    ebias_grad = jnp.sum(grad_pre.astype(jnp.float32), axis=0)
    expand_grad = inner_rows(first_low, grad_pre)
    grad_first = grad_second + lax.psum(
        inner_cols(grad_pre, expand_proj).astype(jnp.bfloat16), "tensor"
    ).astype(jnp.float32)
    grad_mix, again_grad, ashift_grad = norm_backward(
        grad_first, first_normed, first_recip, attn_gain_f
    )
    obias_grad = jnp.sum(grad_mix, axis=0)
    grad_mix_low = grad_mix.astype(jnp.bfloat16)
    oproj_grad = inner_rows(attended, grad_mix_low)
    grad_attended = inner_cols(grad_mix_low, output_proj).astype(jnp.bfloat16)
    grad_heads = split_heads(grad_attended)

    def head_backward(state, group):
        query_head, key_head, value_head, grad_head, log_sum = group
        scores = cross_scores(query_head, key_head) * scale
        attn_probs = jnp.where(same_seg, jnp.exp(scores - log_sum), 0.0)
        grad_probs = cross_scores(grad_head, value_head)
        row_dot = jnp.sum(attn_probs * grad_probs, axis=1, keepdims=True)
        grad_scores = (attn_probs * (grad_probs - row_dot)).astype(jnp.bfloat16)
        grad_query = spread_apply(grad_scores, key_head) * scale
        grad_key = spread_transpose(grad_scores, query_head) * scale
        grad_value = spread_transpose(attn_probs.astype(jnp.bfloat16), grad_head)
        return (state, (grad_query, grad_key, grad_value))

    query_back, key_back, value_back = lax.scan(
        head_backward, None, (query_heads, key_heads, value_heads, grad_heads, log_sums)
    )[1]
    grad_queries = join_heads(query_back).astype(jnp.bfloat16)
    key_sum, value_sum = (
        lax.psum_scatter(
            join_heads(key_back).astype(jnp.bfloat16), "ctx", scatter_dimension=0, tiled=True
        ).astype(jnp.float32),
        lax.psum_scatter(
            join_heads(value_back).astype(jnp.bfloat16), "ctx", scatter_dimension=0, tiled=True
        ).astype(jnp.float32),
    )
    grad_keys = key_sum.astype(jnp.bfloat16)
    grad_values = value_sum.astype(jnp.bfloat16)
    qbias_grad = jnp.sum(grad_queries.astype(jnp.float32), axis=0)
    vbias_grad = jnp.sum(grad_values.astype(jnp.float32), axis=0)
    query_grad = inner_rows(inputs, grad_queries)
    key_grad = inner_rows(inputs, grad_keys)
    value_grad = inner_rows(inputs, grad_values)
    back_terms = (
        inner_cols(grad_queries, query_proj)
        + inner_cols(grad_keys, key_proj)
        + inner_cols(grad_values, value_proj)
    )
    input_grad = grad_mix + lax.psum(back_terms.astype(jnp.bfloat16), "tensor").astype(jnp.float32)
    (
        query_grad,
        key_grad,
        value_grad,
        qbias_grad,
        vbias_grad,
        oproj_grad,
        obias_grad,
        again_grad,
        ashift_grad,
        expand_grad,
        ebias_grad,
        shrink_grad,
        sbias_grad,
        fgain_grad,
        fshift_grad,
    ) = lax.psum(
        (
            query_grad,
            key_grad,
            value_grad,
            qbias_grad,
            vbias_grad,
            oproj_grad,
            obias_grad,
            again_grad,
            ashift_grad,
            expand_grad,
            ebias_grad,
            shrink_grad,
            sbias_grad,
            fgain_grad,
            fshift_grad,
        ),
        ("dp", "ctx"),
    )
    return (
        output.astype(jnp.bfloat16),
        input_grad,
        query_grad,
        key_grad,
        value_grad,
        qbias_grad,
        vbias_grad,
        oproj_grad,
        obias_grad,
        again_grad,
        ashift_grad,
        expand_grad,
        ebias_grad,
        shrink_grad,
        sbias_grad,
        fgain_grad,
        fshift_grad,
    )


def solution(mesh):
    in_specs = (
        P(("dp", "ctx"), None),
        P("dp", "ctx"),
        P(None, "tensor"),
        P(None, "tensor"),
        P(None, "tensor"),
        P("tensor"),
        P("tensor"),
        P("tensor", None),
        P(),
        P(),
        P(),
        P(None, "tensor"),
        P("tensor"),
        P("tensor", None),
        P(),
        P(),
        P(),
        P(("dp", "ctx"), None),
    )
    out_specs = (
        P(("dp", "ctx"), None),
        P(("dp", "ctx"), None),
        P(None, "tensor"),
        P(None, "tensor"),
        P(None, "tensor"),
        P("tensor"),
        P("tensor"),
        P("tensor", None),
        P(),
        P(),
        P(),
        P(None, "tensor"),
        P("tensor"),
        P("tensor", None),
        P(),
        P(),
        P(),
    )
    return jax.shard_map(body, mesh=mesh, in_specs=in_specs, out_specs=out_specs, check_vma=False)
```

profile of v0, /device:TPU:0, one launch (start us, length us, event | category | flops | bytes accessed | tf_op | source)
XLA Modules:
  0.0 743.4 jit_solution(2113761524882374570)
XLA Ops:
  7.3 2.8 convolution_convert_fusion.4
  10.2 2.4 fusion.62
  12.7 13.7 %all-gather = bf16[1,2048]{1,0:T(2,128)(2,1)S(1)} all-gather(bf16[1,512]{1,0:T(2,128)(2,1)S(1)} %get-tuple-element.288), channel_id=2, replica_groups=mesh['dp'=4,'ctx'=4,'tensor'=2] {'ctx'}, dimensions={1}, use_global_device_ids=true | all-gather | bytes 5120 | tf_op jit(solution)/shard_map/all_gather | solution.py:84
  29.1 21.0 %all-gather.4.cloned.1.call-done = bf16[2048,384]{1,0:T(8,128)(2,1)} async-done(((bf16[512,384]{1,0:T(8,128)(2,1)}), bf16[2048,384]{1,0:T(8,128)(2,1)}) %all-gather.4.cloned.1.call-update) | async-done | bytes 1572880 | tf_op jit(solution)/shard_map/all_gather | solution.py:82
  50.1 2.6 copy.43
  52.6 4.1 copy.45
  56.8 31.5 %all-gather.6.cloned.1.call-done = bf16[2048,384]{1,0:T(8,128)(2,1)} async-done(((bf16[512,384]{1,0:T(8,128)(2,1)}), bf16[2048,384]{1,0:T(8,128)(2,1)}) %all-gather.6.cloned.1.call-update) | async-done | bytes 1572880 | tf_op jit(solution)/shard_map/all_gather | solution.py:83
  88.2 2.6 copy.44
  90.8 4.1 copy.46
  94.9 38.4 %while.28 = (s32[]{:T(128)}, bf16[6,512,64]{1,2,0:T(8,128)(2,1)S(1)}, f32[6,512,1]{1,2,0:T(1,128)}, bf16[6,512,64]{2,1,0:T(8,128)(2,1)}, bf16[6,2048,64]{2,1,0:T...) while((s32[]{:T(128)}, ...), condition=%wide.region_3.4_spmd.clone, body=%wide.region_0.3_spmd.clone.sunk | while | flops 286260736 | bytes 13946985 | solution.py:111
  94.9 2.0 fusion.132
  98.1 2.6 fusion.134
  101.3 2.0 fusion.132
  104.5 2.6 fusion.134
  107.7 2.0 fusion.132
  110.9 2.6 fusion.134
  114.1 2.0 fusion.132
  117.3 2.6 fusion.134
  120.5 2.0 fusion.132
  123.7 2.6 fusion.134
  126.9 2.0 fusion.132
  130.1 2.6 fusion.134
  133.3 2.7 convolution_convert_fusion.2
  140.6 28.8 %all-reduce.8.cloned.1.call-done = bf16[512,768]{1,0:T(8,128)(2,1)} async-done(((bf16[512,768]{1,0:T(8,128)(2,1)}), bf16[512,768]{1,0:T(8,128)(2,1)}) %all-reduce.8.cloned.1.call-update) | async-done | bytes 786448 | tf_op jit(solution)/shard_map/psum | solution.py:113
  171.5 9.5 %multiply_convert_fusion.1 = (bf16[512,1536]{1,0:T(8,128)(2,1)S(1)}, f32[512,1536]{1,0:T(8,128)}, f32[512,1536]{1,0:T(8,128)}) fusion(f32[1536]{0:T(1024)S(1)} %copy-done.41, bf16[768,1536]{1,0:T(8,128)(2,1)S(1)} %copy-done, f32[768]{0:T(1024)S(1)} %copy-done.38, f32[768]{0:T(1024)S(1)} %copy-done.23, f32[512]{0:T(512)S(1)} %add_rsqrt_fusion.1, ...), kind=kOutput, calls=%fused_computation.62 | convolution fusion | flops 1263403008 | bytes 11815936 | tf_op jit(solution)/shard_map/dot_general | solution.py:14
  182.3 2.3 convolution_convert_fusion.1
  184.8 34.2 %all-reduce.10.cloned.1.call-done = bf16[512,768]{1,0:T(8,128)(2,1)} async-done(((bf16[512,768]{1,0:T(8,128)(2,1)}), bf16[512,768]{1,0:T(8,128)(2,1)}) %all-reduce.10.cloned.1.call-update) | async-done | bytes 786448 | tf_op jit(solution)/shard_map/psum | solution.py:126
  219.1 2.2 fusion.78
  225.0 2.9 convert_reduce_fusion
  229.1 2.3 convolution_convert_fusion
  231.5 34.4 %all-reduce.12.cloned.1.call-done = bf16[512,768]{1,0:T(8,128)(2,1)} async-done(((bf16[512,768]{1,0:T(8,128)(2,1)}), bf16[512,768]{1,0:T(8,128)(2,1)}) %all-reduce.12.cloned.1.call-update) | async-done | bytes 786448 | tf_op jit(solution)/shard_map/psum | solution.py:145
  265.9 3.5 multiply_reduce_fusion.1
  273.7 70.0 %while.29 = (s32[]{:T(128)}, bf16[6,512,64]{1,2,0:T(8,128)(2,1)S(1)}, bf16[6,2048,64]{1,2,0:T(8,128)(2,1)}, bf16[6,2048,64]{1,2,0:T(8,128)(2,1)}, bf16[6,512,64]...) while((s32[]{:T(128)}, ...), condition=%wide.region_17.18_spmd.clone, body=%wide.region_15.17_spmd.clone.sunk | while | flops 681737728 | bytes 34759808 | solution.py:169
  276.2 2.6 multiply_reduce_fusion.7
  279.3 2.1 fusion.146
  283.2 2.2 fusion.145
  287.9 2.6 multiply_reduce_fusion.7
  290.9 2.2 fusion.146
  294.9 2.1 fusion.145
  299.5 2.6 multiply_reduce_fusion.7
  302.6 2.2 fusion.146
  306.6 2.1 fusion.145
  311.2 2.6 multiply_reduce_fusion.7
  314.3 2.2 fusion.146
  318.2 2.1 fusion.145
  322.9 2.6 multiply_reduce_fusion.7
  325.9 2.2 fusion.146
  329.9 2.1 fusion.145
  334.5 2.6 multiply_reduce_fusion.7
  337.6 2.1 fusion.146
  341.5 2.1 fusion.145
  345.1 5.1 fusion.67
  350.3 3.8 fusion.73
  357.4 21.8 %reduce-scatter.3.cloned.1.call-done = bf16[512,384]{0,1:T(8,128)(2,1)} async-done(((bf16[2048,384]{0,1:T(8,128)(2,1)}), bf16[512,384]{0,1:T(8,128)(2,1)}) %reduce-scatter.3.cloned.1.call-update) | async-done | bytes 393232 | tf_op jit(solution)/shard_map/reduce_scatter | solution.py:174
  379.1 3.0 fusion.82
  382.1 33.8 %reduce-scatter.5.cloned.1.call-done = bf16[512,384]{0,1:T(8,128)(2,1)} async-done(((bf16[2048,384]{0,1:T(8,128)(2,1)}), bf16[512,384]{0,1:T(8,128)(2,1)}) %reduce-scatter.5.cloned.1.call-update) | async-done | bytes 393232 | tf_op jit(solution)/shard_map/reduce_scatter | solution.py:177
  415.8 3.5 add_convert_fusion.1
  424.7 61.2 %all-reduce = (f32[384]{0:T(512)}, f32[384]{0:T(512)}, f32[768]{0:T(1024)}, f32[768]{0:T(1024)}, f32[768]{0:T(1024)}, /*index=5*/f32[1536]{0:T(1024)}, f32[768]{0:T(1024)}, f32[768]{0:T(1024)}, f32[768]{0:T(1024)}) all-reduce(f32[384]{0:T(512)S(1)} %reduce_sum.182, ...), channel_id=1, replica_groups=mesh['dp'=4,'ctx'=4,'tensor'=2] {'dp','ctx'}, use_global_device_ids=true, to_apply=%region_25.26 | all-reduce | flops 6912 | bytes 55296 | tf_op jit(solution)/shard_map/psum | solution.py:210
  485.9 2.4 convert_add_fusion
  488.3 231.7 %all-reduce.16.cloned.1.call-done = (f32[768,384]{0,1:T(8,128)}, f32[768,384]{0,1:T(8,128)}, f32[768,384]{0,1:T(8,128)}, f32[384,768]{1,0:T(8,128)}, f32[768,1536]{1,0:T(8,128)}, /*index=5*/f32[1536,768]{1,0:T(8,128)}) async-done(((f32[768,384]{0,1:T(8,128)}, f32[768,384]{0,1:T(8,128)}, f32[768,384]{0,1:T(8,128)}, f32[384,768]{1,0:T(8,128)}, f32[768,1536]{1,0:T(8,128)}, /*index=5*/f32[1536,768]{1,0:T(8,128)}), ...) | async-done | bytes 14155792 | tf_op jit(solution)/shard_map/psum | solution.py:210
  720.1 2.7 copy.50
  722.8 2.7 copy.51
  728.0 5.5 copy.92
  733.5 2.4 copy.93
  (219 shorter events, 72.9 us)
Async XLA Ops:
  7.2 164.2 %copy-start = (bf16[768,1536]{1,0:T(8,128)(2,1)S(1)}, bf16[768,1536]{1,0:T(8,128)(2,1)}, u32[]{:S(2)}) copy-start(bf16[768,1536]{1,0:T(8,128)(2,1)} %param.33) | copy-start | bytes 7077892
  7.2 3.0 copy-start.2
  7.2 2.9 copy-start.47
  7.2 5.4 copy-start.48
  7.2 5.4 copy-start.43
  7.2 42.8 %all-gather.4.cloned.1.call-start = ((), (), s32[]{:S(2)}) async-start(), calls=%async_computation.2 | async-start | bytes 1966080 | tf_op jit(solution)/shard_map/all_gather | solution.py:82
  10.1 78.1 %all-gather.6.cloned.1.call-start = ((), (), s32[]{:S(2)}) async-start(), calls=%async_computation.3 | async-start | bytes 1966080 | tf_op jit(solution)/shard_map/all_gather | solution.py:83
  12.6 156.8 %all-reduce.8.cloned.1.call-start = ((), (), s32[]{:S(2)}) async-start(), calls=%async_computation.4 | async-start | bytes 1572864 | tf_op jit(solution)/shard_map/psum | solution.py:113
  133.3 38.1 %copy-start.12 = (bf16[6,512,64]{1,2,0:T(8,128)(2,1)}, bf16[6,512,64]{1,2,0:T(8,128)(2,1)S(1)}, u32[]{:S(2)}) copy-start(bf16[6,512,64]{1,2,0:T(8,128)(2,1)S(1)} %get-tuple-element.109) | copy-start | bytes 1179652
  136.0 83.0 %all-reduce.10.cloned.1.call-start = ((), (), s32[]{:S(2)}) async-start(), calls=%async_computation.5 | async-start | bytes 1572864 | tf_op jit(solution)/shard_map/psum | solution.py:126
  169.4 1.6 copy-start.8
  169.4 2.1 copy-start.23
  169.4 2.1 copy-start.38
  169.4 2.1 copy-start.41
  170.9 10.1 %copy-start.26 = (f32[512]{0:T(512)}, f32[512]{0:T(512)S(1)}, u32[]{:S(2)}) copy-start(f32[512]{0:T(512)S(1)} %broadcast_multiply_fusion.5) | copy-start | bytes 6148
  171.5 9.6 %copy-start.29 = (f32[512]{0:T(512)}, f32[512]{0:T(512)S(1)}, u32[]{:S(2)}) copy-start(f32[512]{0:T(512)S(1)} %add_rsqrt_fusion.1) | copy-start | bytes 6148
  171.5 10.7 %copy-start.49 = (bf16[1536,768]{1,0:T(8,128)(2,1)S(1)}, bf16[1536,768]{1,0:T(8,128)(2,1)}, u32[]{:S(2)}) copy-start(bf16[1536,768]{1,0:T(8,128)(2,1)} %param.35) | copy-start | bytes 7077892
  181.0 1.2 copy-start.16
  182.2 2.6 copy-start.44
  182.2 2.6 copy-start.45
  182.2 2.6 copy-start.46
  182.2 36.8 %copy-start.24 = (f32[768]{0:T(1024)S(1)}, f32[768]{0:T(1024)}, u32[]{:S(2)}) copy-start(f32[768]{0:T(1024)} %convert_element_type.185) | copy-start | bytes 9220
  182.2 36.8 %copy-start.27 = (f32[512]{0:T(512)S(1)}, f32[512]{0:T(512)}, u32[]{:S(2)}) copy-start(f32[512]{0:T(512)} %copy-done.26) | copy-start | bytes 6148
  182.2 36.8 %copy-start.30 = (f32[512]{0:T(512)S(1)}, f32[512]{0:T(512)}, u32[]{:S(2)}) copy-start(f32[512]{0:T(512)} %copy-done.29) | copy-start | bytes 6148
  182.2 36.8 %copy-start.39 = (f32[768]{0:T(1024)S(1)}, f32[768]{0:T(1024)}, u32[]{:S(2)}) copy-start(f32[768]{0:T(1024)} %convert_element_type.186) | copy-start | bytes 9220
  184.5 81.4 %all-reduce.12.cloned.1.call-start = ((), (), s32[]{:S(2)}) async-start(), calls=%async_computation.6 | async-start | bytes 1572864 | tf_op jit(solution)/shard_map/psum | solution.py:145
  219.0 2.6 copy-start.14
  221.3 3.4 copy-start.54
  221.6 3.1 copy-start.53
  223.0 2.1 copy-start.50
  224.7 3.2 copy-start.3
  227.9 1.2 copy-start.51
  231.4 38.0 %copy-start.4 = (f32[512,768]{1,0:T(8,128)S(1)}, f32[512,768]{1,0:T(8,128)}, u32[]{:S(2)}) copy-start(f32[512,768]{1,0:T(8,128)} %copy-done.3) | copy-start | bytes 4718596
  231.4 38.0 %copy-start.9 = (bf16[512,768]{1,0:T(8,128)(2,1)S(1)}, bf16[512,768]{1,0:T(8,128)(2,1)}, u32[]{:S(2)}) copy-start(bf16[512,768]{1,0:T(8,128)(2,1)} %all-reduce.8.cloned.1.call-done) | copy-start | bytes 2359300
  231.4 147.7 %reduce-scatter.3.cloned.1.call-start = ((), (), s32[]{:S(2)}) async-start(), calls=%async_computation.7 | async-start | bytes 1966080 | tf_op jit(solution)/shard_map/reduce_scatter | solution.py:174
  265.9 3.6 copy-start.15
  269.5 2.5 copy-start.17
  270.8 1.1 copy-start.6
  343.7 1.4 copy-start.5
  343.7 72.2 %reduce-scatter.5.cloned.1.call-start = ((), (), s32[]{:S(2)}) async-start(), calls=%async_computation.8 | async-start | bytes 1966080 | tf_op jit(solution)/shard_map/reduce_scatter | solution.py:177
  344.4 5.8 copy-start.10
  344.4 5.8 copy-start.25
  344.5 5.8 copy-start.28
  344.5 5.7 copy-start.31
  344.5 141.4 %all-reduce.14.cloned.1.call-start = ((), (), s32[]{:S(2)}) async-start(), calls=%async_computation.9 | async-start | bytes 1572864 | tf_op jit(solution)/shard_map/psum | solution.py:193
  345.1 5.2 copy-start.40
  345.1 5.2 copy-start.52
  350.2 3.9 copy-start.22
  354.1 1.8 copy-start.7
  354.1 1.8 copy-start.13
  357.4 58.5 %copy-start.21 = (bf16[768,384]{1,0:T(8,128)(2,1)S(1)}, bf16[768,384]{1,0:T(8,128)(2,1)}, u32[]{:S(2)}) copy-start(bf16[768,384]{1,0:T(8,128)(2,1)} %param.26) | copy-start | bytes 1769476
  419.4 1.6 copy-start.11
  419.4 3.0 copy-start.18
  419.4 300.7 %all-reduce.16.cloned.1.call-start = ((), (), s32[]{:S(2)}) async-start(), calls=%async_computation.10 | async-start | bytes 28311552 | tf_op jit(solution)/shard_map/psum | solution.py:210
  423.9 0.7 copy-start.34
  423.9 0.7 copy-start.35
  423.9 0.7 copy-start.36
  423.9 0.7 copy-start.37
  423.9 0.7 copy-start.42
  720.1 5.5 copy-start.20
  722.8 4.1 copy-start.19
  727.0 6.5 slice-start
  728.0 5.5 slice-start.1
  733.5 3.4 copy-start.1
  (2 other events, 1.4 us)
Sparse Core Ops, SparseCore 0:
  10.2 39.8 all-gather.3
  52.2 35.9 all-gather.5
  136.1 33.1 all-reduce.7
  184.7 34.3 all-reduce.9
  231.5 34.3 all-reduce.11
  343.8 35.2 reduce-scatter.2
  381.5 34.2 reduce-scatter.4
  419.5 33.2 all-reduce.13
  459.1 260.8 all-reduce.15
where the time goes:
time: 746 us; the launch traced here: 743 us
  waiting for transfers between devices  438 us (59%)
  matrix products  141 us (19%)
  blocking collectives  74.9 us (10%)
  local copies, waits for them, and re-layouts  44.8 us (6%)
  other arithmetic  29.9 us (4%)
  between operations  14.4 us (2%)
    psum x1, waiting for transfers between devices, body(): lax.psum((query_grad, key_grad, value_grad, qbias_grad, vbias_grad, oproj...  232 us
    psum x1, blocking collectives, body(): lax.psum((query_grad, key_grad, value_grad, qbias_grad, vbias_grad, oproj...  61.2 us
    dot_general x24, matrix products, inner_cols(): lax.dot_general(left, right, contract_cols, preferred_element_type=jnp.fl...  52.3 us
    dot_general x18, matrix products, matmul(): return jnp.dot(left, right, preferred_element_type=jnp.float32)  47.6 us
    dot_general x18, matrix products, inner_rows(): lax.dot_general(left, right, contract_rows, preferred_element_type=jnp.fl...  40.7 us
    psum x1, waiting for transfers between devices, body(): lax.psum(inner_cols(grad_pre, expand_proj).astype(jnp.bfloat16), 'tensor')  34.4 us
    psum x1, waiting for transfers between devices, body(): lax.psum(matmul(hidden, shrink_proj).astype(jnp.bfloat16), 'tensor')  34.2 us
    reduce_scatter x1, waiting for transfers between devices, body(): lax.psum_scatter(join_heads(value_back).astype(jnp.bfloat16), 'ctx', scat...  33.8 us
  transfers between devices with their start and end apart: 9, of which 8 were waited for; matrix products, arithmetic and copies ran while one was open for 5% of the time, Pallas kernels for 0%

commit v1 on v0

--- a/solution.py
+++ b/solution.py
@@ -8,6 +8,11 @@
 masked = -1e30
 contract_rows = (((0,), (0,)), ((), ()))
 contract_cols = (((1,), (1,)), ((), ()))
+
+
+def tiled_gather(array, axis, dim):
+    copies = jnp.concatenate([array] * lax.axis_size(axis), axis=dim)
+    return lax.all_to_all(copies, axis, dim, dim, tiled=True)
 
 
 def matmul(left, right):
@@ -80,7 +85,7 @@
     values = (matmul(inputs, value_proj) + value_bias.astype(jnp.float32)).astype(jnp.bfloat16)
     all_keys, all_values, key_ids = (
         lax.all_gather(keys, "ctx", axis=0, tiled=True),
-        lax.all_gather(values, "ctx", axis=0, tiled=True),
+        tiled_gather(values, "ctx", 0),
         lax.all_gather(seg_local.astype(jnp.bfloat16), "ctx", axis=0, tiled=True),
     )
     query_segs = seg_local.astype(jnp.float32)

time: 746 us -> 759 us (1.017)
  waiting for transfers between devices: 438 us -> 386 us
  blocking collectives: 74.9 us -> 124 us
  local copies, waits for them, and re-layouts: 44.8 us -> 52.8 us
    all_gather x1, blocking collectives: 13.7 us -> 62.5 us  [body(): lax.all_gather(seg_local.astype(jnp.bfloat16), 'ctx', axis=0, tiled=True)]
    all_gather x1 -> x0, waiting for transfers between devices: 31.5 us -> none  [body(): lax.all_gather(values, 'ctx', axis=0, tiled=True)]
    all_gather x1, waiting for transfers between devices: 21 us -> 0.01 us  [body(): lax.all_gather(keys, 'ctx', axis=0, tiled=True)]
    unnamed x122 -> x120, local copies, waits for them, and re-layouts: 29.6 us -> 30 us
  transfers between devices with their start and end apart: 9 -> 9, of which waited for: 8 -> 6; matrix products, arithmetic and copies ran while one was open for 5% -> 6% of each run, Pallas kernels for 0% -> 0%
where the time goes in v1:
time: 759 us; the launch traced here: 757 us
  waiting for transfers between devices  386 us (51%)
  matrix products  140 us (18%)
  blocking collectives  124 us (16%)
  local copies, waits for them, and re-layouts  52.8 us (7%)
  other arithmetic  32 us (4%)
  between operations  14.7 us (2%)
    psum x1, waiting for transfers between devices, body(): lax.psum((query_grad, key_grad, value_grad, qbias_grad, vbias_grad, oproj...  231 us
    all_gather x1, blocking collectives, body(): lax.all_gather(seg_local.astype(jnp.bfloat16), 'ctx', axis=0, tiled=True)  62.5 us
    psum x1, blocking collectives, body(): lax.psum((query_grad, key_grad, value_grad, qbias_grad, vbias_grad, oproj...  61.5 us
    dot_general x24, matrix products, inner_cols(): lax.dot_general(left, right, contract_cols, preferred_element_type=jnp.fl...  52.3 us
    dot_general x18, matrix products, matmul(): return jnp.dot(left, right, preferred_element_type=jnp.float32)  46.6 us
    dot_general x18, matrix products, inner_rows(): lax.dot_general(left, right, contract_rows, preferred_element_type=jnp.fl...  40.7 us
    psum x1, waiting for transfers between devices, body(): lax.psum(matmul(hidden, shrink_proj).astype(jnp.bfloat16), 'tensor')  34.4 us
    psum x1, waiting for transfers between devices, body(): lax.psum(inner_cols(grad_pre, expand_proj).astype(jnp.bfloat16), 'tensor')  34.2 us
  transfers between devices with their start and end apart: 9, of which 6 were waited for; matrix products, arithmetic and copies ran while one was open for 6% of the time, Pallas kernels for 0%

profile of v1, /device:TPU:0, one launch (start us, length us, event | category | flops | bytes accessed | tf_op | source)
XLA Modules:
  0.0 756.7 jit_solution(7866176037499462892)
XLA Ops:
  11.2 2.6 copy.54
  13.8 6.5 all-to-all-start
  20.3 2.4 convolution_convert_fusion.4
  22.8 62.5 %all-gather = bf16[1,2048]{1,0:T(2,128)(2,1)S(1)} all-gather(bf16[1,512]{1,0:T(2,128)(2,1)S(1)} %get-tuple-element.324), channel_id=2, replica_groups=mesh['dp'=4,'ctx'=4,'tensor'=2] {'ctx'}, dimensions={1}, use_global_device_ids=true | all-gather | bytes 5120 | tf_op jit(solution)/shard_map/all_gather | solution.py:89
  88.0 3.8 copy.55
  91.8 3.8 reshape.141
  95.6 4.1 copy.57
  99.7 2.6 copy.53
  102.3 4.1 copy.56
  106.4 38.4 %while.28 = (s32[]{:T(128)}, bf16[6,512,64]{1,2,0:T(8,128)(2,1)S(1)}, f32[6,512,1]{1,2,0:T(1,128)}, bf16[6,512,64]{2,1,0:T(8,128)(2,1)}, bf16[6,2048,64]{2,1,0:T...) while((s32[]{:T(128)}, ...), condition=%wide.region_3.4_spmd.clone, body=%wide.region_0.3_spmd.clone.sunk | while | flops 286260736 | bytes 13946985 | solution.py:116
  106.4 2.0 fusion.132
  109.6 2.6 fusion.134
  112.8 2.0 fusion.132
  116.0 2.6 fusion.134
  119.2 2.0 fusion.132
  122.4 2.6 fusion.134
  125.6 2.0 fusion.132
  128.8 2.6 fusion.134
  132.0 2.0 fusion.132
  135.2 2.6 fusion.134
  138.4 2.0 fusion.132
  141.6 2.6 fusion.134
  144.8 2.7 convolution_convert_fusion.2
  152.3 30.3 %all-reduce.8.cloned.1.call-done = bf16[512,768]{1,0:T(8,128)(2,1)} async-done(((bf16[512,768]{1,0:T(8,128)(2,1)}), bf16[512,768]{1,0:T(8,128)(2,1)}) %all-reduce.8.cloned.1.call-update) | async-done | bytes 786448 | tf_op jit(solution)/shard_map/psum | solution.py:118
  184.6 9.5 %multiply_convert_fusion.1 = (bf16[512,1536]{1,0:T(8,128)(2,1)S(1)}, f32[512,1536]{1,0:T(8,128)}, f32[512,1536]{1,0:T(8,128)}) fusion(f32[1536]{0:T(1024)S(1)} %copy-done.41, bf16[768,1536]{1,0:T(8,128)(2,1)S(1)} %copy-done, f32[768]{0:T(1024)S(1)} %copy-done.38, f32[768]{0:T(1024)S(1)} %copy-done.23, f32[512]{0:T(512)S(1)} %add_rsqrt_fusion.1, ...), kind=kOutput, calls=%fused_computation.62 | convolution fusion | flops 1263403008 | bytes 11815936 | tf_op jit(solution)/shard_map/dot_general | solution.py:19
  195.4 2.3 convolution_convert_fusion.1
  197.8 34.4 %all-reduce.10.cloned.1.call-done = bf16[512,768]{1,0:T(8,128)(2,1)} async-done(((bf16[512,768]{1,0:T(8,128)(2,1)}), bf16[512,768]{1,0:T(8,128)(2,1)}) %all-reduce.10.cloned.1.call-update) | async-done | bytes 786448 | tf_op jit(solution)/shard_map/psum | solution.py:131
  232.2 2.2 fusion.78
  238.1 2.9 convert_reduce_fusion
  242.2 2.3 convolution_convert_fusion
  244.8 34.2 %all-reduce.12.cloned.1.call-done = bf16[512,768]{1,0:T(8,128)(2,1)} async-done(((bf16[512,768]{1,0:T(8,128)(2,1)}), bf16[512,768]{1,0:T(8,128)(2,1)}) %all-reduce.12.cloned.1.call-update) | async-done | bytes 786448 | tf_op jit(solution)/shard_map/psum | solution.py:150
  279.0 3.5 multiply_reduce_fusion.1
  286.8 70.0 %while.29 = (s32[]{:T(128)}, bf16[6,512,64]{1,2,0:T(8,128)(2,1)S(1)}, bf16[6,2048,64]{1,2,0:T(8,128)(2,1)}, bf16[6,2048,64]{1,2,0:T(8,128)(2,1)}, bf16[6,512,64]...) while((s32[]{:T(128)}, ...), condition=%wide.region_17.18_spmd.clone, body=%wide.region_15.17_spmd.clone.sunk | while | flops 681737728 | bytes 34759808 | solution.py:174
  289.3 2.6 multiply_reduce_fusion.7
  292.4 2.2 fusion.146
  296.3 2.1 fusion.145
  301.0 2.6 multiply_reduce_fusion.7
  304.0 2.2 fusion.146
  308.0 2.1 fusion.145
  312.6 2.6 multiply_reduce_fusion.7
  315.7 2.2 fusion.146
  319.6 2.1 fusion.145
  324.3 2.6 multiply_reduce_fusion.7
  327.3 2.2 fusion.146
  331.3 2.1 fusion.145
  335.9 2.6 multiply_reduce_fusion.7
  339.0 2.2 fusion.146
  343.0 2.1 fusion.145
  347.6 2.6 multiply_reduce_fusion.7
  350.7 2.2 fusion.146
  354.6 2.1 fusion.145
  358.2 5.1 fusion.67
  363.4 3.8 fusion.73
  370.5 21.8 %reduce-scatter.3.cloned.1.call-done = bf16[512,384]{0,1:T(8,128)(2,1)} async-done(((bf16[2048,384]{0,1:T(8,128)(2,1)}), bf16[512,384]{0,1:T(8,128)(2,1)}) %reduce-scatter.3.cloned.1.call-update) | async-done | bytes 393232 | tf_op jit(solution)/shard_map/reduce_scatter | solution.py:179
  392.2 3.0 fusion.82
  395.2 33.6 %reduce-scatter.5.cloned.1.call-done = bf16[512,384]{0,1:T(8,128)(2,1)} async-done(((bf16[2048,384]{0,1:T(8,128)(2,1)}), bf16[512,384]{0,1:T(8,128)(2,1)}) %reduce-scatter.5.cloned.1.call-update) | async-done | bytes 393232 | tf_op jit(solution)/shard_map/reduce_scatter | solution.py:182
  428.8 3.5 add_convert_fusion.1
  437.9 61.5 %all-reduce = (f32[384]{0:T(512)}, f32[384]{0:T(512)}, f32[768]{0:T(1024)}, f32[768]{0:T(1024)}, f32[768]{0:T(1024)}, /*index=5*/f32[1536]{0:T(1024)}, f32[768]{0:T(1024)}, f32[768]{0:T(1024)}, f32[768]{0:T(1024)}) all-reduce(f32[384]{0:T(512)S(1)} %reduce_sum.182, ...), channel_id=1, replica_groups=mesh['dp'=4,'ctx'=4,'tensor'=2] {'dp','ctx'}, use_global_device_ids=true, to_apply=%region_25.26 | all-reduce | flops 6912 | bytes 55296 | tf_op jit(solution)/shard_map/psum | solution.py:215
  499.4 2.5 convert_add_fusion
  501.8 231.2 %all-reduce.16.cloned.1.call-done = (f32[768,384]{0,1:T(8,128)}, f32[768,384]{0,1:T(8,128)}, f32[768,384]{0,1:T(8,128)}, f32[384,768]{1,0:T(8,128)}, f32[768,1536]{1,0:T(8,128)}, /*index=5*/f32[1536,768]{1,0:T(8,128)}) async-done(((f32[768,384]{0,1:T(8,128)}, f32[768,384]{0,1:T(8,128)}, f32[768,384]{0,1:T(8,128)}, f32[384,768]{1,0:T(8,128)}, f32[768,1536]{1,0:T(8,128)}, /*index=5*/f32[1536,768]{1,0:T(8,128)}), ...) | async-done | bytes 14155792 | tf_op jit(solution)/shard_map/psum | solution.py:215
  733.0 2.7 copy.61
  735.8 2.7 copy.62
  741.0 5.5 copy.103
  746.5 2.4 copy.104
  (219 shorter events, 77.2 us)
Async XLA Ops:
  7.2 177.4 %copy-start = (bf16[768,1536]{1,0:T(8,128)(2,1)S(1)}, bf16[768,1536]{1,0:T(8,128)(2,1)}, u32[]{:S(2)}) copy-start(bf16[768,1536]{1,0:T(8,128)(2,1)} %param.33) | copy-start | bytes 7077892
  13.8 6.5 copy-start.2
  13.8 8.9 %copy-start.47 = (bf16[384]{0:T(512)(128)(2,1)S(1)}, bf16[384]{0:T(512)(128)(2,1)}, u32[]{:S(2)}) copy-start(bf16[384]{0:T(512)(128)(2,1)} %param.27) | copy-start | bytes 2308
  13.8 9.0 %copy-start.43 = (s32[1,512]{1,0:T(1,128)S(1)}, s32[1,512]{1,0:T(1,128)}, u32[]{:S(2)}) copy-start(s32[1,512]{1,0:T(1,128)} %param.23) | copy-start | bytes 6148
  13.8 74.2 %all-to-all-start = ((bf16[4,512,384]{1,2,0:T(8,128)(2,1)}), bf16[4,512,384]{1,2,0:T(8,128)(2,1)}, u32[]{:S(2)}, u32[]{:S(2)}) async-start(bf16[4,512,384]{1,2,0:T(8,128)(2,1)} %copy.54), calls=%async_computation | async-start | bytes 3145728 | tf_op jit(solution)/shard_map/all_to_all | solution.py:15
  20.2 79.4 %all-gather.3.cloned.1.call-start = ((), (), s32[]{:S(2)}) async-start(), calls=%async_computation.3 | async-start | bytes 1966080 | tf_op jit(solution)/shard_map/all_gather | solution.py:87
  22.7 159.9 %all-reduce.8.cloned.1.call-start = ((), (), s32[]{:S(2)}) async-start(), calls=%async_computation.4 | async-start | bytes 1572864 | tf_op jit(solution)/shard_map/psum | solution.py:118
  144.8 39.7 %copy-start.12 = (bf16[6,512,64]{1,2,0:T(8,128)(2,1)}, bf16[6,512,64]{1,2,0:T(8,128)(2,1)S(1)}, u32[]{:S(2)}) copy-start(bf16[6,512,64]{1,2,0:T(8,128)(2,1)S(1)} %get-tuple-element.109) | copy-start | bytes 1179652
  147.5 84.6 %all-reduce.10.cloned.1.call-start = ((), (), s32[]{:S(2)}) async-start(), calls=%async_computation.5 | async-start | bytes 1572864 | tf_op jit(solution)/shard_map/psum | solution.py:131
  182.5 1.6 copy-start.8
  182.5 2.1 copy-start.23
  182.5 2.1 copy-start.38
  182.5 2.1 copy-start.41
  184.1 10.1 %copy-start.26 = (f32[512]{0:T(512)}, f32[512]{0:T(512)S(1)}, u32[]{:S(2)}) copy-start(f32[512]{0:T(512)S(1)} %broadcast_multiply_fusion.5) | copy-start | bytes 6148
  184.6 9.5 %copy-start.29 = (f32[512]{0:T(512)}, f32[512]{0:T(512)S(1)}, u32[]{:S(2)}) copy-start(f32[512]{0:T(512)S(1)} %add_rsqrt_fusion.1) | copy-start | bytes 6148
  184.6 10.7 %copy-start.48 = (bf16[1536,768]{1,0:T(8,128)(2,1)S(1)}, bf16[1536,768]{1,0:T(8,128)(2,1)}, u32[]{:S(2)}) copy-start(bf16[1536,768]{1,0:T(8,128)(2,1)} %param.35) | copy-start | bytes 7077892
  194.1 1.1 copy-start.16
  195.3 2.4 copy-start.44
  195.3 2.4 copy-start.45
  195.3 2.4 copy-start.46
  195.3 36.8 %copy-start.24 = (f32[768]{0:T(1024)S(1)}, f32[768]{0:T(1024)}, u32[]{:S(2)}) copy-start(f32[768]{0:T(1024)} %convert_element_type.185) | copy-start | bytes 9220
  195.3 36.8 %copy-start.27 = (f32[512]{0:T(512)S(1)}, f32[512]{0:T(512)}, u32[]{:S(2)}) copy-start(f32[512]{0:T(512)} %copy-done.26) | copy-start | bytes 6148
  195.3 36.8 %copy-start.30 = (f32[512]{0:T(512)S(1)}, f32[512]{0:T(512)}, u32[]{:S(2)}) copy-start(f32[512]{0:T(512)} %copy-done.29) | copy-start | bytes 6148
  195.3 36.8 %copy-start.39 = (f32[768]{0:T(1024)S(1)}, f32[768]{0:T(1024)}, u32[]{:S(2)}) copy-start(f32[768]{0:T(1024)} %convert_element_type.186) | copy-start | bytes 9220
  197.6 81.4 %all-reduce.12.cloned.1.call-start = ((), (), s32[]{:S(2)}) async-start(), calls=%async_computation.6 | async-start | bytes 1572864 | tf_op jit(solution)/shard_map/psum | solution.py:150
  232.1 2.6 copy-start.14
  234.4 3.4 copy-start.53
  234.7 3.1 copy-start.52
  236.1 2.1 copy-start.49
  237.8 3.2 copy-start.3
  241.0 1.2 copy-start.50
  244.5 38.0 %copy-start.4 = (f32[512,768]{1,0:T(8,128)S(1)}, f32[512,768]{1,0:T(8,128)}, u32[]{:S(2)}) copy-start(f32[512,768]{1,0:T(8,128)} %copy-done.3) | copy-start | bytes 4718596
  244.5 38.0 %copy-start.9 = (bf16[512,768]{1,0:T(8,128)(2,1)S(1)}, bf16[512,768]{1,0:T(8,128)(2,1)}, u32[]{:S(2)}) copy-start(bf16[512,768]{1,0:T(8,128)(2,1)} %all-reduce.8.cloned.1.call-done) | copy-start | bytes 2359300
  244.5 147.7 %reduce-scatter.3.cloned.1.call-start = ((), (), s32[]{:S(2)}) async-start(), calls=%async_computation.7 | async-start | bytes 1966080 | tf_op jit(solution)/shard_map/reduce_scatter | solution.py:179
  279.0 3.6 copy-start.15
  282.6 2.5 copy-start.17
  283.9 1.1 copy-start.6
  356.8 1.4 copy-start.5
  356.8 72.0 %reduce-scatter.5.cloned.1.call-start = ((), (), s32[]{:S(2)}) async-start(), calls=%async_computation.8 | async-start | bytes 1966080 | tf_op jit(solution)/shard_map/reduce_scatter | solution.py:182
  357.4 5.9 copy-start.10
  357.4 5.9 copy-start.25
  357.4 5.9 copy-start.28
  357.4 5.9 copy-start.31
  357.4 142.0 %all-reduce.14.cloned.1.call-start = ((), (), s32[]{:S(2)}) async-start(), calls=%async_computation.9 | async-start | bytes 1572864 | tf_op jit(solution)/shard_map/psum | solution.py:198
  358.2 5.2 copy-start.40
  358.2 5.2 copy-start.51
  363.4 3.9 copy-start.22
  367.2 1.8 copy-start.7
  367.2 1.8 copy-start.13
  370.5 58.3 %copy-start.21 = (bf16[768,384]{1,0:T(8,128)(2,1)S(1)}, bf16[768,384]{1,0:T(8,128)(2,1)}, u32[]{:S(2)}) copy-start(bf16[768,384]{1,0:T(8,128)(2,1)} %param.26) | copy-start | bytes 1769476
  432.3 1.8 copy-start.11
  432.4 3.3 copy-start.18
  432.4 300.7 %all-reduce.16.cloned.1.call-start = ((), (), s32[]{:S(2)}) async-start(), calls=%async_computation.10 | async-start | bytes 28311552 | tf_op jit(solution)/shard_map/psum | solution.py:215
  437.1 0.7 copy-start.33
  437.2 0.7 copy-start.34
  437.2 0.7 copy-start.35
  437.2 0.7 copy-start.36
  437.2 0.7 copy-start.37
  437.2 0.7 copy-start.42
  733.0 5.5 copy-start.20
  735.8 4.1 copy-start.19
  739.9 6.5 slice-start
  741.0 5.5 slice-start.1
  746.5 3.4 copy-start.1
  (1 other events, 0.7 us)
Sparse Core Ops, SparseCore 0:
  23.2 59.2 all-gather.2
  147.6 34.8 all-reduce.7
  197.8 34.3 all-reduce.9
  244.6 34.3 all-reduce.11
  356.9 35.2 reduce-scatter.2
  394.5 34.2 reduce-scatter.4
  432.5 33.2 all-reduce.13
  472.1 260.9 all-reduce.15
